TPU v7x, 32 devices: a whole 2x2x4 slice. The times are simulated.
32 devices in a mesh: rep: 1, seq: 16 (over z, y, core), head: 2 (over x).
Axes of the slice: x: 2, y: 2, z: 4, core: 2. Of those that a mesh axis runs over, the one named last changes fastest.
Arguments:
- states: bfloat16 [256, 8192], P('rep', 'seq'), may hold values from -6 to 6
- w_query: bfloat16 [8192, 8192], P('seq', 'head'), may hold values from -0.0625 to 0.0625
- w_key: bfloat16 [8192, 1024], P('seq', 'head'), may hold values from -0.3125 to 0.3125
- w_value: bfloat16 [8192, 1024], P('seq', 'head'), may hold values from -0.25 to 0.25
- w_out: bfloat16 [8192, 8192], P('head', 'seq'), may hold values from -0.09375 to 0.09375
- key_cache: bfloat16 [2, 8192, 1024], P('rep', 'seq', 'head'), may hold values from -480 to 480
- value_cache: bfloat16 [2, 8192, 1024], P('rep', 'seq', 'head'), may hold values from -24 to 24
- parents: int32 [2, 128], P('rep'), may hold values from 0 to 126, as said below
- cache_lengths: int32 [2], P('rep'), may hold values from 2048 to 8192, as said below
Outputs:
- attended: bfloat16 [256, 8192], P('rep', ('seq', 'head'))
Inputs may be any that keep to these rules, and one draw needn't show every extreme that they name: parents[t, 0] = 0, parents[t, i] < i for i >= 1, and the last node's parent is node 126. `cache_lengths`: at least one sequence fills all 8192 positions.
All inputs are finite; a program needn't handle non-finite values.
Results may differ from a plain program's by a relative error of at most 0.014.
The roundings to bfloat16 on the way count: a program that leaves them out, or rounds other values in their place, can miss the bound.
Values may be sent and summed in bfloat16 or wider, within the bound.
No kernel may reach another device: no remote copies, remote signals or barrier semaphores. Data moves between devices by JAX's collectives and lax.ppermute only.
A program may use at most 320 MiB of HBM per device.

v0:
```python
import jax
import jax.numpy as jnp
from jax import lax
from jax.sharding import PartitionSpec as P

HEAD_DIM = 128
rope_base = 500000.0
neg_big = -1e30


def ancestry(parents):
    count = parents.shape[1]
    ident = jnp.eye(count, dtype=jnp.float32)
    onehot = (parents[:, :, None] == jnp.arange(count, dtype=jnp.int32)[None, None, :]).astype(
        jnp.float32
    )
    reach = jnp.minimum(ident[None] + onehot, 1.0)
    for level in range(max(1, (count - 1).bit_length())):
        reach = jnp.minimum(
            jnp.einsum("tij,tjk->tik", reach, reach, precision=lax.Precision.HIGHEST), 1.0
        )
    return reach


def rotate(values, position):
    count = values.shape[0]
    half = HEAD_DIM // 2
    shaped = values.reshape(count, -1, HEAD_DIM)
    freq = rope_base ** (-(jnp.arange(half, dtype=jnp.float32) * 2.0 / HEAD_DIM))
    angle = position[:, None] * freq[None, :]
    cosine = jnp.cos(angle)[:, None, :]
    sine = jnp.sin(angle)[:, None, :]
    first = shaped[..., :half]
    second = shaped[..., half:]
    turned = jnp.concatenate([first * cosine - second * sine, second * cosine + first * sine], -1)
    return turned.reshape(count, -1)


def combine(left, right):
    top = jnp.maximum(left[0], right[0])
    scale_left = jnp.exp(left[0] - top)
    scale_right = jnp.exp(right[0] - top)
    return (
        top,
        left[1] * scale_left + right[1] * scale_right,
        left[2] * scale_left[..., None] + right[2] * scale_right[..., None],
    )


def cache_state(query, keys, values, length, offset):
    total = keys.shape[0]
    block = min(total, 2048)
    count = total // block
    rows_here, kv_local, group, width = query.shape
    scale = width ** (-0.5)
    keys = keys.reshape(count, block, kv_local, width)
    values = values.reshape(count, block, kv_local, width)

    def step(carry, inputs):
        key_block, value_block, first = inputs
        valid = offset + first + jnp.arange(block, dtype=jnp.int32) < length
        scores = (
            jnp.einsum("rkgd,nkd->rkgn", query, key_block, preferred_element_type=jnp.float32)
            * scale
        )
        scores = jnp.where(valid, scores, neg_big)
        top = jnp.maximum(carry[0], jnp.max(scores, -1))
        weights = jnp.where(valid, jnp.exp(scores - top[..., None]), 0.0)
        shrink = jnp.exp(carry[0] - top)
        mass = carry[1] * shrink + jnp.sum(weights, -1)
        acc = carry[2] * shrink[..., None] + jnp.einsum(
            "rkgn,nkd->rkgd",
            weights.astype(jnp.bfloat16),
            value_block,
            preferred_element_type=jnp.float32,
        )
        return ((top, mass, acc), None)

    init = (
        jnp.full((rows_here, kv_local, group), neg_big, jnp.float32),
        jnp.zeros((rows_here, kv_local, group), jnp.float32),
        jnp.zeros((rows_here, kv_local, group, width), jnp.float32),
    )
    firsts = jnp.arange(count, dtype=jnp.int32) * block
    state, _ = lax.scan(step, init, (keys, values, firsts))
    return state


def tree_state(query, new_keys, new_values, allowed):
    rows_here, kv_local, group, width = query.shape
    scale = width ** (-0.5)
    keys = new_keys.reshape(-1, kv_local, width)
    values = new_values.reshape(-1, kv_local, width)
    mask = allowed[:, None, None, :]
    scores = jnp.einsum("rkgd,nkd->rkgn", query, keys, preferred_element_type=jnp.float32) * scale
    scores = jnp.where(mask, scores, neg_big)
    top = jnp.max(scores, -1)
    weights = jnp.where(mask, jnp.exp(scores - top[..., None]), 0.0)
    acc = jnp.einsum(
        "rkgn,nkd->rkgd", weights.astype(jnp.bfloat16), values, preferred_element_type=jnp.float32
    )
    return (top, jnp.sum(weights, -1), acc)


def local(states, w_query, w_key, w_value, w_out, key_cache, value_cache, parents, cache_lengths):
    trees, tree_rows = parents.shape
    rows = trees * tree_rows
    kv_local = key_cache.shape[2] // HEAD_DIM
    heads_local = w_query.shape[1] // HEAD_DIM
    group = heads_local // kv_local
    reach = ancestry(parents)
    position = (cache_lengths.astype(jnp.float32)[:, None] + jnp.sum(reach, -1) - 1.0).reshape(-1)
    allowed = (jnp.eye(trees, dtype=jnp.float32)[:, None, :, None] * reach[:, :, None, :]).reshape(
        rows, rows
    ) > 0.5
    q_part = jnp.dot(states, w_query, preferred_element_type=jnp.float32)
    k_part = jnp.dot(states, w_key, preferred_element_type=jnp.float32)
    v_part = jnp.dot(states, w_value, preferred_element_type=jnp.float32)
    q_raw, k_raw, v_raw = lax.psum((q_part, k_part, v_part), "seq")
    queries = rotate(q_raw, position).astype(jnp.bfloat16)
    new_keys = rotate(k_raw, position).astype(jnp.bfloat16)
    new_values = v_raw.astype(jnp.bfloat16)
    query_heads = queries.reshape(rows, kv_local, group, HEAD_DIM)
    offset = lax.axis_index("seq") * key_cache.shape[1]
    parts_list = []
    for tree in range(trees):
        parts_list.append(
            cache_state(
                query_heads[tree * tree_rows : (tree + 1) * tree_rows],
                key_cache[tree],
                value_cache[tree],
                cache_lengths[tree],
                offset,
            )
        )
    peak = jnp.concatenate([item[0] for item in parts_list], 0)
    mass = jnp.concatenate([item[1] for item in parts_list], 0)
    acc = jnp.concatenate([item[2] for item in parts_list], 0)
    summit = lax.pmax(peak, "seq")
    factor = jnp.exp(peak - summit)
    mass_share, acc_share = (
        lax.psum_scatter(mass * factor, "seq", scatter_dimension=0, tiled=True),
        lax.psum_scatter(acc * factor[..., None], "seq", scatter_dimension=0, tiled=True),
    )
    share = mass_share.shape[0]
    first_row = lax.axis_index("seq") * share
    summit_share = lax.dynamic_slice_in_dim(summit, first_row, share)
    query_share = lax.dynamic_slice_in_dim(query_heads, first_row, share)
    allowed_share = lax.dynamic_slice_in_dim(allowed, first_row, share)
    total = combine(
        (summit_share, mass_share, acc_share),
        tree_state(query_share, new_keys, new_values, allowed_share),
    )
    attention_share = (total[2] / total[1][..., None]).reshape(share, -1).astype(jnp.bfloat16)
    attention = lax.all_gather(attention_share, "seq", axis=0, tiled=True)
    partial_value = jnp.dot(attention, w_out, preferred_element_type=jnp.float32)
    return lax.psum_scatter(partial_value, "head", scatter_dimension=1, tiled=True).astype(
        jnp.bfloat16
    )


def solution(mesh):
    placed = (
        P("rep", "seq"),
        P("seq", "head"),
        P("seq", "head"),
        P("seq", "head"),
        P("head", "seq"),
        P("rep", "seq", "head"),
        P("rep", "seq", "head"),
        P("rep", None),
        P("rep"),
    )
    return jax.shard_map(
        local, mesh=mesh, in_specs=placed, out_specs=P("rep", ("seq", "head")), check_vma=False
    )
```

profile of v0, /device:TPU:0, one launch (start us, length us, event | category | flops | bytes accessed | tf_op | source)
XLA Modules:
  0.0 412.9 jit_solution(16273453118756324011)
XLA Ops:
  6.5 1.0 copy-done
  7.6 1.2 convolution_bitcast_fusion.1
  8.8 0.9 copy.84
  9.7 3.5 convolution_bitcast_fusion
  13.2 2.7 copy.76
  16.0 1.1 copy-done.6
  17.3 0.6 fusion.66
  18.0 1.0 copy.74
  19.2 1.0 copy.72
  20.4 1.8 fusion.47
  22.2 0.4 convolution_minimum_fusion.6
  22.6 0.3 convolution_minimum_fusion.5
  23.7 0.3 convolution_minimum_fusion.1
  24.0 0.4 fusion.67
  24.4 0.5 multiply_cosine_fusion
  25.0 110.8 %all-reduce.4.cloned.1.call-done = (f32[256,4,128]{2,0,1:T(8,128)}, f32[256,32,128]{2,1,0:T(8,128)}) async-done(((f32[256,4,128]{2,0,1:T(8,128)}, f32[256,32,128]{2,1,0:T(8,128)}), (f32[256,4,128]{2,0,1:T(8,128)}, f32[256,32,128]{2,1,0:T(8,128)})) %all-reduce.4.cloned.1.call-update) | async-done | bytes 4718608 | tf_op jit(solution)/shard_map/psum | solution.py:119
  135.7 4.8 %multiply_subtract_fusion = (bf16[256,32,64]{2,1,0:T(8,128)(2,1)S(1)}, bf16[256,32,64]{2,1,0:T(8,128)(2,1)S(1)}) fusion(f32[256,32,128]{2,1,0:T(8,128)} %get-tuple-element.40, f32[256,64]{1,0:T(8,128)S(1)} %get-tuple-element.81, f32[256,64]{1,0:T(8,128)S(1)} %get-tuple-element.80), kind=kLoop, calls=%fused_computation.17 | loop fusion | flops 4194304 | bytes 6422528 | tf_op jit(solution)/shard_map/sub | solution.py:35
  140.6 1.2 maximum_convert_fusion
  141.8 0.4 fusion.63
  142.1 0.4 copy.40
  142.5 1.3 bitcast_reduce_fusion
  143.9 3.1 fusion.6
  147.1 0.6 fusion.60
  147.7 0.4 copy.35
  148.1 1.3 bitcast_reduce_fusion.1
  149.5 2.4 fusion.4
  151.9 0.8 copy-done.3
  152.7 0.6 fusion.59
  153.3 60.0 %pmax.7 = f32[256,4,8]{0,2,1:T(8,128)S(1)} all-reduce(f32[256,4,8]{0,2,1:T(8,128)S(1)} %pad_maximum_fusion), channel_id=1, replica_groups=mesh['rep'=1,'seq'=16,'head'=2] {'seq'}, use_global_device_ids=true, to_apply=%region_4.5 | all-reduce | flops 8192 | bytes 65536 | tf_op jit(solution)/shard_map/pmax | solution.py:139
  213.3 0.6 fusion.43
  213.9 0.8 copy.69
  215.0 5.7 %bitcast_add_fusion = f32[128,4,8,128]{3,0,2,1:T(8,128)S(1)} fusion(bf16[512,4,128,1]{0,2,3,1:T(8,128)(2,1)S(1)} %bitcast.140, f32[4,128,8,512]{3,1,2,0:T(8,128)} %copy-done.2, f32[128,4,8]{0,2,1:T(8,128)S(1)} %broadcast_maximum_fusion, pred[512]{0:T(512)(128)(4,1)} %copy-done.19, f32[128,4,8]{0,2,1:T(8,128)} %get-tuple-element.79), kind=kOutput, calls=%fused_computation.25 | convolution fusion | flops 547880960 | bytes 11043328 | tf_op jit(solution)/shard_map/while/body/eval_jaxpr/rkgn,nkd->rkgd/dot_general | solution.py:71
  220.7 5.5 %bitcast_add_fusion.1 = f32[128,4,8,128]{3,0,2,1:T(8,128)S(1)} fusion(bf16[512,4,128,1]{0,2,3,1:T(8,128)(2,1)S(1)} %bitcast.139, f32[4,128,8,512]{3,1,2,0:T(8,128)} %copy-done.3, f32[128,4,8]{0,2,1:T(8,128)S(1)} %copy-done.11, pred[512]{0:T(512)(128)(4,1)S(1)} %copy-done.18, f32[128,4,8]{0,2,1:T(8,128)S(1)} %copy-done.16), kind=kOutput, calls=%fused_computation.26 | convolution fusion | flops 547880960 | bytes 11043328 | tf_op jit(solution)/shard_map/while/body/eval_jaxpr/rkgn,nkd->rkgd/dot_general | solution.py:71
  226.2 2.6 maximum_multiply_fusion
  229.2 0.6 copy-done.4
  229.8 2.1 fusion.69
  231.9 63.7 %all-reduce.5 = bf16[256,512]{1,0:T(8,128)(2,1)S(1)} all-reduce(f32[256,512]{1,0:T(8,128)} %fusion.69), channel_id=1, replica_groups=mesh['rep'=1,'seq'=16,'head'=2] {'seq'}, use_global_device_ids=true, to_apply=%region_8.9 | all-reduce | flops 131072 | bytes 786432 | tf_op jit(solution)/shard_map/psum | solution.py:119
  295.6 0.8 reshape.143
  296.4 0.8 copy.46
  297.5 0.4 fusion.68
  298.2 0.8 copy.70
  299.1 44.5 %reduce-scatter.6.cloned.1.call-done = f32[16,4,8,128]{3,0,2,1:T(8,128)} async-done(((f32[256,4,8,128]{3,0,2,1:T(8,128)}), f32[16,4,8,128]{3,0,2,1:T(8,128)}) %reduce-scatter.6.cloned.1.call-update) | async-done | bytes 262160 | tf_op jit(solution)/shard_map/reduce_scatter | solution.py:143
  343.5 1.4 fusion.25
  344.9 0.7 copy.86
  345.7 40.6 %all-gather.2.cloned.1.call-done = bf16[256,4096]{1,0:T(8,128)(2,1)} async-done(((bf16[16,4096]{1,0:T(8,128)(2,1)}), bf16[256,4096]{1,0:T(8,128)(2,1)}) %all-gather.2.cloned.1.call-update) | async-done | bytes 2097168 | tf_op jit(solution)/shard_map/all_gather | solution.py:155
  386.4 4.9 %fusion.70 = f32[256,512]{1,0:T(8,128)} fusion(bf16[256,4096]{1,0:T(8,128)(2,1)} %all-gather.2.cloned.1.call-done, bf16[4096,512]{1,0:T(8,128)(2,1)} %param.13), kind=kOutput, calls=%fused_computation.111 | convolution fusion | flops 1073741824 | bytes 6815744 | tf_op jit(solution)/shard_map/dot_general | solution.py:156
  391.3 13.5 %reduce-scatter.8.cloned.1.call-done = f32[256,256]{1,0:T(8,128)} async-done(((f32[256,512]{1,0:T(8,128)}), f32[256,256]{1,0:T(8,128)}) %reduce-scatter.8.cloned.1.call-update) | async-done | bytes 262160 | tf_op jit(solution)/shard_map/reduce_scatter | solution.py:157
  404.8 1.6 convert_element_type.65
  (73 shorter events, 3.0 us)
Async XLA Ops:
  6.5 1.0 copy-start
  6.5 129.2 %all-reduce.4.cloned.1.call-start = ((), (), s32[]{:S(2)}) async-start(), calls=%async_computation.7 | async-start | bytes 9437184 | tf_op jit(solution)/shard_map/psum | solution.py:119
  16.0 1.2 copy-start.6
  16.0 1.3 copy-start.20
  16.0 1.9 copy-start.7
  16.0 6.2 %copy-start.21 = (s32[2,128]{1,0:T(2,128)S(1)}, s32[2,128]{1,0:T(2,128)}, u32[]{:S(2)}) copy-start(s32[2,128]{1,0:T(2,128)} %param.16) | copy-start | bytes 3076
  16.0 282.2 %reduce-scatter.10.cloned.1.call-start = ((), (), s32[]{:S(2)}) async-start(), calls=%async_computation.6 | async-start | bytes 139264
  22.2 120.3 %copy-start.19 = (pred[512]{0:T(512)(128)(4,1)}, pred[512]{0:T(512)(128)(4,1)S(1)}, u32[]{:S(2)}) copy-start(pred[512]{0:T(512)(128)(4,1)S(1)} %get-tuple-element.92) | copy-start | bytes 1540
  143.9 3.2 copy-start.2
  143.9 4.3 %copy-start.17 = (pred[512]{0:T(512)(128)(4,1)S(1)}, pred[512]{0:T(512)(128)(4,1)}, u32[]{:S(2)}) copy-start(pred[512]{0:T(512)(128)(4,1)} %get-tuple-element.93) | copy-start | bytes 1540
  149.5 3.2 copy-start.3
  149.5 63.8 %copy-start.10 = (f32[128,4,8]{0,2,1:T(8,128)}, f32[128,4,8]{0,2,1:T(8,128)S(1)}, u32[]{:S(2)}) copy-start(f32[128,4,8]{0,2,1:T(8,128)S(1)} %broadcast_maximum_fusion.1) | copy-start | bytes 49156
  149.5 63.8 %copy-start.15 = (f32[128,4,8]{0,2,1:T(8,128)S(1)}, f32[128,4,8]{0,2,1:T(8,128)}, u32[]{:S(2)}) copy-start(f32[128,4,8]{0,2,1:T(8,128)} %get-tuple-element.78) | copy-start | bytes 49156
  149.5 65.4 %copy-start.9 = (bf16[1,512,512]{1,2,0:T(8,128)(2,1)S(1)}, bf16[1,512,512]{1,2,0:T(8,128)(2,1)}, u32[]{:S(2)}) copy-start(bf16[1,512,512]{1,2,0:T(8,128)(2,1)} %copy.74) | copy-start | bytes 1572868
  213.3 1.6 copy-start.12
  214.7 128.8 %reduce-scatter.6.cloned.1.call-start = ((), (), s32[]{:S(2)}) async-start(), calls=%async_computation.3 | async-start | bytes 4456448 | tf_op jit(solution)/shard_map/reduce_scatter | solution.py:143
  214.9 5.7 %copy-start.8 = (bf16[1,512,512]{1,2,0:T(8,128)(2,1)S(1)}, bf16[1,512,512]{1,2,0:T(8,128)(2,1)}, u32[]{:S(2)}) copy-start(bf16[1,512,512]{1,2,0:T(8,128)(2,1)} %copy.72) | copy-start | bytes 1572868
  215.0 5.7 %copy-start.11 = (f32[128,4,8]{0,2,1:T(8,128)S(1)}, f32[128,4,8]{0,2,1:T(8,128)}, u32[]{:S(2)}) copy-start(f32[128,4,8]{0,2,1:T(8,128)} %copy-done.10) | copy-start | bytes 49156
  215.0 5.7 %copy-start.16 = (f32[128,4,8]{0,2,1:T(8,128)S(1)}, f32[128,4,8]{0,2,1:T(8,128)}, u32[]{:S(2)}) copy-start(f32[128,4,8]{0,2,1:T(8,128)} %get-tuple-element.77) | copy-start | bytes 49156
  215.0 5.7 %copy-start.18 = (pred[512]{0:T(512)(128)(4,1)S(1)}, pred[512]{0:T(512)(128)(4,1)}, u32[]{:S(2)}) copy-start(pred[512]{0:T(512)(128)(4,1)} %get-tuple-element.93) | copy-start | bytes 1540
  220.7 5.5 %copy-start.14 = (f32[256,4,8]{0,2,1:T(8,128)S(1)}, f32[256,4,8]{0,2,1:T(8,128)}, u32[]{:S(2)}) copy-start(f32[256,4,8]{0,2,1:T(8,128)} %get-tuple-element.54) | copy-start | bytes 98308
  228.8 1.0 copy-start.4
  228.8 68.4 %copy-start.5 = (f32[256,4,128]{2,0,1:T(8,128)S(1)}, f32[256,4,128]{2,0,1:T(8,128)}, u32[]{:S(2)}) copy-start(f32[256,4,128]{2,0,1:T(8,128)} %get-tuple-element.39) | copy-start | bytes 1572868
  228.8 157.5 %all-gather.2.cloned.1.call-start = ((), (), s32[]{:S(2)}) async-start(), calls=%async_computation.4 | async-start | bytes 2228224 | tf_op jit(solution)/shard_map/all_gather | solution.py:155
  295.6 3.3 copy-start.13
  345.7 60.7 %copy-start.1 = (bf16[512,512]{1,0:T(8,128)(2,1)S(1)}, bf16[512,512]{1,0:T(8,128)(2,1)}, u32[]{:S(2)}) copy-start(bf16[512,512]{1,0:T(8,128)(2,1)} %param.11) | copy-start | bytes 1572868
  345.7 59.1 %reduce-scatter.8.cloned.1.call-start = ((), (), s32[]{:S(2)}) async-start(), calls=%async_computation.5 | async-start | bytes 786432 | tf_op jit(solution)/shard_map/reduce_scatter | solution.py:157
Sparse Core Ops, SparseCore 0:
  16.1 119.5 all-reduce.3
  214.8 52.9 reduce-scatter.9
  271.7 71.8 reduce-scatter.5
  345.8 40.5 all-gather.1
  391.4 13.3 reduce-scatter.7
where the time goes:
time: 414 us; the launch traced here: 413 us
  waiting for transfers between devices  209 us (50%)
  blocking collectives  124 us (30%)
  matrix products  29.4 us (7%)
  other arithmetic  20.9 us (5%)
  local copies, waits for them, and re-layouts  15.5 us (4%)
  between operations  13.6 us (3%)
    psum x1, waiting for transfers between devices, local(): q_raw, k_raw, v_raw = lax.psum((q_part, k_part, v_part), 'seq')  111 us
    psum x1, blocking collectives, local(): q_raw, k_raw, v_raw = lax.psum((q_part, k_part, v_part), 'seq')  63.7 us
    pmax x1, blocking collectives, local(): summit = lax.pmax(peak, 'seq')  60 us
    reduce_scatter x1, waiting for transfers between devices, local(): lax.psum_scatter(acc * factor[..., None], 'seq', scatter_dimension=0, til...  44.5 us
    all_gather x1, waiting for transfers between devices, local(): attention = lax.all_gather(attention_share, 'seq', axis=0, tiled=True)  40.6 us
    reduce_scatter x1, waiting for transfers between devices, local(): lax.psum_scatter(partial_value, 'head', scatter_dimension=1, tiled=True)  13.5 us
    unnamed x53, local copies, waits for them, and re-layouts  11.1 us
    dot_general x2, matrix products, step(): jnp.einsum('rkgn,nkd->rkgd', weights.astype(jnp.bfloat16), value_block, p...  11.1 us
  transfers between devices with their start and end apart: 5, of which 4 were waited for; matrix products, arithmetic and copies ran while one was open for 7% of the time, Pallas kernels for 0%

commit v1 on v0

--- a/solution.py
+++ b/solution.py
@@ -152,7 +152,12 @@
         tree_state(query_share, new_keys, new_values, allowed_share),
     )
     attention_share = (total[2] / total[1][..., None]).reshape(share, -1).astype(jnp.bfloat16)
-    attention = lax.all_gather(attention_share, "seq", axis=0, tiled=True)
+    ring = [attention_share]
+    for hop in range(15):
+        ring.append(lax.ppermute(ring[-1], "seq", [(dev, (dev + 1) % 16) for dev in range(16)]))
+    attention = jnp.roll(
+        jnp.concatenate(ring[::-1], axis=0), (lax.axis_index("seq") + 1) * ring[0].shape[0], axis=0
+    )
     partial_value = jnp.dot(attention, w_out, preferred_element_type=jnp.float32)
     return lax.psum_scatter(partial_value, "head", scatter_dimension=1, tiled=True).astype(
         jnp.bfloat16

time: 414 us -> 475 us (1.15)
  waiting for transfers between devices: 209 us -> 273 us
    ppermute x0 -> x15, waiting for transfers between devices: none -> 106 us  [local(): lax.ppermute(ring[-1], 'seq', [(dev, (dev + 1) % 16) for dev in range(16)])]
    all_gather x1 -> x0, waiting for transfers between devices: 40.6 us -> none  [local(): attention = lax.all_gather(attention_share, 'seq', axis=0, tiled=True)]
    unnamed x53 -> x86, local copies, waits for them, and re-layouts: 11.1 us -> 11 us
  transfers between devices with their start and end apart: 5 -> 19, of which waited for: 4 -> 18; matrix products, arithmetic and copies ran while one was open for 7% -> 6% of each run, Pallas kernels for 0% -> 0%
where the time goes in v1:
time: 475 us; the launch traced here: 474 us
  waiting for transfers between devices  273 us (57%)
  blocking collectives  124 us (26%)
  matrix products  26.6 us (6%)
  other arithmetic  20.8 us (4%)
  local copies, waits for them, and re-layouts  15.5 us (3%)
  between operations  13.9 us (3%)
    psum x1, waiting for transfers between devices, local(): q_raw, k_raw, v_raw = lax.psum((q_part, k_part, v_part), 'seq')  111 us
    ppermute x15, waiting for transfers between devices, local(): lax.ppermute(ring[-1], 'seq', [(dev, (dev + 1) % 16) for dev in range(16)])  106 us
    psum x1, blocking collectives, local(): q_raw, k_raw, v_raw = lax.psum((q_part, k_part, v_part), 'seq')  63.8 us
    pmax x1, blocking collectives, local(): summit = lax.pmax(peak, 'seq')  60 us
    reduce_scatter x1, waiting for transfers between devices, local(): lax.psum_scatter(acc * factor[..., None], 'seq', scatter_dimension=0, til...  44.3 us
    reduce_scatter x1, waiting for transfers between devices, local(): lax.psum_scatter(partial_value, 'head', scatter_dimension=1, tiled=True)  12 us
    dot_general x2, matrix products, step(): jnp.einsum('rkgn,nkd->rkgd', weights.astype(jnp.bfloat16), value_block, p...  11.2 us
    unnamed x86, local copies, waits for them, and re-layouts  11 us
  transfers between devices with their start and end apart: 19, of which 18 were waited for; matrix products, arithmetic and copies ran while one was open for 6% of the time, Pallas kernels for 0%

profile of v1, /device:TPU:0, one launch (start us, length us, event | category | flops | bytes accessed | tf_op | source)
XLA Modules:
  0.0 474.5 jit_solution(10311876408813483553)
XLA Ops:
  6.5 1.0 copy-done
  7.6 1.2 convolution_bitcast_fusion.1
  8.8 0.9 copy.88
  9.7 3.5 convolution_bitcast_fusion
  13.3 2.8 copy.76
  16.1 1.1 copy-done.6
  18.0 1.0 copy.74
  19.3 1.0 copy.72
  20.5 1.8 fusion.49
  25.1 110.8 %all-reduce.4.cloned.1.call-done = (f32[256,4,128]{2,0,1:T(8,128)}, f32[256,32,128]{2,1,0:T(8,128)}) async-done(((f32[256,4,128]{2,0,1:T(8,128)}, f32[256,32,128]{2,1,0:T(8,128)}), (f32[256,4,128]{2,0,1:T(8,128)}, f32[256,32,128]{2,1,0:T(8,128)})) %all-reduce.4.cloned.1.call-update) | async-done | bytes 4718608 | tf_op jit(solution)/shard_map/psum | solution.py:119
  135.8 4.8 %multiply_subtract_fusion = (bf16[256,32,64]{2,1,0:T(8,128)(2,1)S(1)}, bf16[256,32,64]{2,1,0:T(8,128)(2,1)S(1)}) fusion(f32[256,32,128]{2,1,0:T(8,128)} %get-tuple-element.40, f32[256,64]{1,0:T(8,128)S(1)} %get-tuple-element.81, f32[256,64]{1,0:T(8,128)S(1)} %get-tuple-element.80), kind=kLoop, calls=%fused_computation.17 | loop fusion | flops 4194304 | bytes 6422528 | tf_op jit(solution)/shard_map/sub | solution.py:35
  140.7 1.2 maximum_convert_fusion
  142.6 1.3 bitcast_reduce_fusion
  144.0 3.0 fusion.6
  147.2 0.6 fusion.63
  148.2 1.3 bitcast_reduce_fusion.1
  149.6 2.4 fusion.4
  152.0 0.8 copy-done.3
  153.4 60.0 %pmax.7 = f32[256,4,8]{0,2,1:T(8,128)S(1)} all-reduce(f32[256,4,8]{0,2,1:T(8,128)S(1)} %pad_maximum_fusion), channel_id=1, replica_groups=mesh['rep'=1,'seq'=16,'head'=2] {'seq'}, use_global_device_ids=true, to_apply=%region_4.5 | all-reduce | flops 8192 | bytes 65536 | tf_op jit(solution)/shard_map/pmax | solution.py:139
  214.0 0.8 copy.69
  215.1 5.7 %bitcast_add_fusion = f32[128,4,8,128]{3,0,2,1:T(8,128)S(1)} fusion(bf16[512,4,128,1]{0,2,3,1:T(8,128)(2,1)S(1)} %bitcast.146, f32[4,128,8,512]{3,1,2,0:T(8,128)} %copy-done.2, f32[128,4,8]{0,2,1:T(8,128)S(1)} %broadcast_maximum_fusion, pred[512]{0:T(512)(128)(4,1)} %copy-done.19, f32[128,4,8]{0,2,1:T(8,128)} %get-tuple-element.79), kind=kOutput, calls=%fused_computation.25 | convolution fusion | flops 547880960 | bytes 11043328 | tf_op jit(solution)/shard_map/while/body/eval_jaxpr/rkgn,nkd->rkgd/dot_general | solution.py:71
  220.9 5.5 %bitcast_add_fusion.1 = f32[128,4,8,128]{3,0,2,1:T(8,128)S(1)} fusion(bf16[512,4,128,1]{0,2,3,1:T(8,128)(2,1)S(1)} %bitcast.145, f32[4,128,8,512]{3,1,2,0:T(8,128)} %copy-done.3, f32[128,4,8]{0,2,1:T(8,128)S(1)} %copy-done.11, pred[512]{0:T(512)(128)(4,1)S(1)} %copy-done.18, f32[128,4,8]{0,2,1:T(8,128)S(1)} %copy-done.16), kind=kOutput, calls=%fused_computation.26 | convolution fusion | flops 547880960 | bytes 11043328 | tf_op jit(solution)/shard_map/while/body/eval_jaxpr/rkgn,nkd->rkgd/dot_general | solution.py:71
  226.4 2.6 maximum_multiply_fusion
  229.9 2.2 fusion.72
  232.1 63.8 %all-reduce.5 = bf16[256,512]{1,0:T(8,128)(2,1)S(1)} all-reduce(f32[256,512]{1,0:T(8,128)} %fusion.72), channel_id=1, replica_groups=mesh['rep'=1,'seq'=16,'head'=2] {'seq'}, use_global_device_ids=true, to_apply=%region_8.9 | all-reduce | flops 131072 | bytes 786432 | tf_op jit(solution)/shard_map/psum | solution.py:119
  295.9 0.8 reshape.143
  296.7 0.8 copy.46
  298.4 0.8 copy.70
  299.3 44.3 %reduce-scatter.6.cloned.1.call-done = f32[16,4,8,128]{3,0,2,1:T(8,128)} async-done(((f32[256,4,8,128]{3,0,2,1:T(8,128)}), f32[16,4,8,128]{3,0,2,1:T(8,128)}) %reduce-scatter.6.cloned.1.call-update) | async-done | bytes 262160 | tf_op jit(solution)/shard_map/reduce_scatter | solution.py:143
  343.6 1.4 fusion.27
  345.2 7.1 %collective-permute-done = bf16[16,4096]{1,0:T(8,128)(2,1)S(1)} collective-permute-done((bf16[16,4096]{1,0:T(8,128)(2,1)S(1)}, bf16[16,4096]{1,0:T(8,128)(2,1)S(1)}, u32[]{:S(2)}, u32[]{:S(2)}) %collective-permute-start) | collective-permute-done | bytes 131104 | tf_op jit(solution)/shard_map/ppermute | solution.py:157
  352.2 7.1 %collective-permute-done.1 = bf16[16,4096]{1,0:T(8,128)(2,1)S(1)} collective-permute-done((bf16[16,4096]{1,0:T(8,128)(2,1)S(1)}, bf16[16,4096]{1,0:T(8,128)(2,1)S(1)}, u32[]{:S(2)}, u32[]{:S(2)}) %collective-permute-start.1) | collective-permute-done | bytes 131104 | tf_op jit(solution)/shard_map/ppermute | solution.py:157
  359.3 7.1 %collective-permute-done.2 = bf16[16,4096]{1,0:T(8,128)(2,1)S(1)} collective-permute-done((bf16[16,4096]{1,0:T(8,128)(2,1)S(1)}, bf16[16,4096]{1,0:T(8,128)(2,1)S(1)}, u32[]{:S(2)}, u32[]{:S(2)}) %collective-permute-start.2) | collective-permute-done | bytes 131104 | tf_op jit(solution)/shard_map/ppermute | solution.py:157
  366.4 7.1 %collective-permute-done.3 = bf16[16,4096]{1,0:T(8,128)(2,1)S(1)} collective-permute-done((bf16[16,4096]{1,0:T(8,128)(2,1)S(1)}, bf16[16,4096]{1,0:T(8,128)(2,1)S(1)}, u32[]{:S(2)}, u32[]{:S(2)}) %collective-permute-start.3) | collective-permute-done | bytes 131104 | tf_op jit(solution)/shard_map/ppermute | solution.py:157
  373.5 7.1 %collective-permute-done.4 = bf16[16,4096]{1,0:T(8,128)(2,1)S(1)} collective-permute-done((bf16[16,4096]{1,0:T(8,128)(2,1)S(1)}, bf16[16,4096]{1,0:T(8,128)(2,1)S(1)}, u32[]{:S(2)}, u32[]{:S(2)}) %collective-permute-start.4) | collective-permute-done | bytes 131104 | tf_op jit(solution)/shard_map/ppermute | solution.py:157
  380.6 7.1 %collective-permute-done.5 = bf16[16,4096]{1,0:T(8,128)(2,1)S(1)} collective-permute-done((bf16[16,4096]{1,0:T(8,128)(2,1)S(1)}, bf16[16,4096]{1,0:T(8,128)(2,1)S(1)}, u32[]{:S(2)}, u32[]{:S(2)}) %collective-permute-start.5) | collective-permute-done | bytes 131104 | tf_op jit(solution)/shard_map/ppermute | solution.py:157
  387.7 7.1 %collective-permute-done.6 = bf16[16,4096]{1,0:T(8,128)(2,1)S(1)} collective-permute-done((bf16[16,4096]{1,0:T(8,128)(2,1)S(1)}, bf16[16,4096]{1,0:T(8,128)(2,1)S(1)}, u32[]{:S(2)}, u32[]{:S(2)}) %collective-permute-start.6) | collective-permute-done | bytes 131104 | tf_op jit(solution)/shard_map/ppermute | solution.py:157
  394.8 7.1 %collective-permute-done.7 = bf16[16,4096]{1,0:T(8,128)(2,1)S(1)} collective-permute-done((bf16[16,4096]{1,0:T(8,128)(2,1)S(1)}, bf16[16,4096]{1,0:T(8,128)(2,1)S(1)}, u32[]{:S(2)}, u32[]{:S(2)}) %collective-permute-start.7) | collective-permute-done | bytes 131104 | tf_op jit(solution)/shard_map/ppermute | solution.py:157
  401.9 7.1 %collective-permute-done.8 = bf16[16,4096]{1,0:T(8,128)(2,1)S(1)} collective-permute-done((bf16[16,4096]{1,0:T(8,128)(2,1)S(1)}, bf16[16,4096]{1,0:T(8,128)(2,1)S(1)}, u32[]{:S(2)}, u32[]{:S(2)}) %collective-permute-start.8) | collective-permute-done | bytes 131104 | tf_op jit(solution)/shard_map/ppermute | solution.py:157
  409.0 7.1 %collective-permute-done.9 = bf16[16,4096]{1,0:T(8,128)(2,1)S(1)} collective-permute-done((bf16[16,4096]{1,0:T(8,128)(2,1)S(1)}, bf16[16,4096]{1,0:T(8,128)(2,1)S(1)}, u32[]{:S(2)}, u32[]{:S(2)}) %collective-permute-start.9) | collective-permute-done | bytes 131104 | tf_op jit(solution)/shard_map/ppermute | solution.py:157
  416.1 7.1 %collective-permute-done.10 = bf16[16,4096]{1,0:T(8,128)(2,1)S(1)} collective-permute-done((bf16[16,4096]{1,0:T(8,128)(2,1)S(1)}, bf16[16,4096]{1,0:T(8,128)(2,1)S(1)}, u32[]{:S(2)}, u32[]{:S(2)}) %collective-permute-start.10) | collective-permute-done | bytes 131104 | tf_op jit(solution)/shard_map/ppermute | solution.py:157
  423.1 7.1 %collective-permute-done.11 = bf16[16,4096]{1,0:T(8,128)(2,1)S(1)} collective-permute-done((bf16[16,4096]{1,0:T(8,128)(2,1)S(1)}, bf16[16,4096]{1,0:T(8,128)(2,1)S(1)}, u32[]{:S(2)}, u32[]{:S(2)}) %collective-permute-start.11) | collective-permute-done | bytes 131104 | tf_op jit(solution)/shard_map/ppermute | solution.py:157
  430.2 7.1 %collective-permute-done.12 = bf16[16,4096]{1,0:T(8,128)(2,1)S(1)} collective-permute-done((bf16[16,4096]{1,0:T(8,128)(2,1)S(1)}, bf16[16,4096]{1,0:T(8,128)(2,1)S(1)}, u32[]{:S(2)}, u32[]{:S(2)}) %collective-permute-start.12) | collective-permute-done | bytes 131104 | tf_op jit(solution)/shard_map/ppermute | solution.py:157
  437.3 7.1 %collective-permute-done.13 = bf16[16,4096]{1,0:T(8,128)(2,1)S(1)} collective-permute-done((bf16[16,4096]{1,0:T(8,128)(2,1)S(1)}, bf16[16,4096]{1,0:T(8,128)(2,1)S(1)}, u32[]{:S(2)}, u32[]{:S(2)}) %collective-permute-start.13) | collective-permute-done | bytes 131104 | tf_op jit(solution)/shard_map/ppermute | solution.py:157
  444.4 7.1 %collective-permute-done.14 = bf16[16,4096]{1,0:T(8,128)(2,1)S(1)} collective-permute-done((bf16[16,4096]{1,0:T(8,128)(2,1)S(1)}, bf16[16,4096]{1,0:T(8,128)(2,1)S(1)}, u32[]{:S(2)}, u32[]{:S(2)}) %collective-permute-start.14) | collective-permute-done | bytes 131104 | tf_op jit(solution)/shard_map/ppermute | solution.py:157
  452.2 2.1 fusion.16
  454.3 12.0 %reduce-scatter.8.cloned.1.call-done = f32[256,256]{1,0:T(8,128)} async-done(((f32[256,512]{1,0:T(8,128)}), f32[256,256]{1,0:T(8,128)}) %reduce-scatter.8.cloned.1.call-update) | async-done | bytes 262160 | tf_op jit(solution)/shard_map/reduce_scatter | solution.py:162
  466.3 1.6 convert_element_type.65
  (134 shorter events, 9.3 us)
Async XLA Ops:
  6.5 1.0 copy-start
  6.5 129.3 %all-reduce.4.cloned.1.call-start = ((), (), s32[]{:S(2)}) async-start(), calls=%async_computation.6 | async-start | bytes 9437184 | tf_op jit(solution)/shard_map/psum | solution.py:119
  16.0 1.2 copy-start.6
  16.0 1.3 copy-start.20
  16.0 1.9 copy-start.7
  16.1 6.3 %copy-start.21 = (s32[2,128]{1,0:T(2,128)S(1)}, s32[2,128]{1,0:T(2,128)}, u32[]{:S(2)}) copy-start(s32[2,128]{1,0:T(2,128)} %param.16) | copy-start | bytes 3076
  16.1 282.4 %reduce-scatter.10.cloned.1.call-start = ((), (), s32[]{:S(2)}) async-start(), calls=%async_computation.5 | async-start | bytes 139264
  22.3 120.3 %copy-start.19 = (pred[512]{0:T(512)(128)(4,1)}, pred[512]{0:T(512)(128)(4,1)S(1)}, u32[]{:S(2)}) copy-start(pred[512]{0:T(512)(128)(4,1)S(1)} %get-tuple-element.92) | copy-start | bytes 1540
  143.9 3.2 copy-start.2
  144.0 4.2 copy-start.17
  149.5 3.3 copy-start.3
  149.6 63.9 %copy-start.10 = (f32[128,4,8]{0,2,1:T(8,128)}, f32[128,4,8]{0,2,1:T(8,128)S(1)}, u32[]{:S(2)}) copy-start(f32[128,4,8]{0,2,1:T(8,128)S(1)} %broadcast_maximum_fusion.1) | copy-start | bytes 49156
  149.6 63.8 %copy-start.15 = (f32[128,4,8]{0,2,1:T(8,128)S(1)}, f32[128,4,8]{0,2,1:T(8,128)}, u32[]{:S(2)}) copy-start(f32[128,4,8]{0,2,1:T(8,128)} %get-tuple-element.78) | copy-start | bytes 49156
  149.6 65.5 %copy-start.9 = (bf16[1,512,512]{1,2,0:T(8,128)(2,1)S(1)}, bf16[1,512,512]{1,2,0:T(8,128)(2,1)}, u32[]{:S(2)}) copy-start(bf16[1,512,512]{1,2,0:T(8,128)(2,1)} %copy.74) | copy-start | bytes 1572868
  213.4 1.6 copy-start.12
  214.8 128.8 %reduce-scatter.6.cloned.1.call-start = ((), (), s32[]{:S(2)}) async-start(), calls=%async_computation.3 | async-start | bytes 4456448 | tf_op jit(solution)/shard_map/reduce_scatter | solution.py:143
  215.1 5.8 %copy-start.8 = (bf16[1,512,512]{1,2,0:T(8,128)(2,1)S(1)}, bf16[1,512,512]{1,2,0:T(8,128)(2,1)}, u32[]{:S(2)}) copy-start(bf16[1,512,512]{1,2,0:T(8,128)(2,1)} %copy.72) | copy-start | bytes 1572868
  215.1 5.8 %copy-start.11 = (f32[128,4,8]{0,2,1:T(8,128)S(1)}, f32[128,4,8]{0,2,1:T(8,128)}, u32[]{:S(2)}) copy-start(f32[128,4,8]{0,2,1:T(8,128)} %copy-done.10) | copy-start | bytes 49156
  215.1 5.8 %copy-start.16 = (f32[128,4,8]{0,2,1:T(8,128)S(1)}, f32[128,4,8]{0,2,1:T(8,128)}, u32[]{:S(2)}) copy-start(f32[128,4,8]{0,2,1:T(8,128)} %get-tuple-element.77) | copy-start | bytes 49156
  215.1 5.8 %copy-start.18 = (pred[512]{0:T(512)(128)(4,1)S(1)}, pred[512]{0:T(512)(128)(4,1)}, u32[]{:S(2)}) copy-start(pred[512]{0:T(512)(128)(4,1)} %get-tuple-element.93) | copy-start | bytes 1540
  220.9 5.5 %copy-start.14 = (f32[256,4,8]{0,2,1:T(8,128)S(1)}, f32[256,4,8]{0,2,1:T(8,128)}, u32[]{:S(2)}) copy-start(f32[256,4,8]{0,2,1:T(8,128)} %get-tuple-element.54) | copy-start | bytes 98308
  229.0 1.0 copy-start.4
  229.0 68.5 %copy-start.5 = (f32[256,4,128]{2,0,1:T(8,128)S(1)}, f32[256,4,128]{2,0,1:T(8,128)}, u32[]{:S(2)}) copy-start(f32[256,4,128]{2,0,1:T(8,128)} %get-tuple-element.39) | copy-start | bytes 1572868
  229.0 237.3 %reduce-scatter.8.cloned.1.call-start = ((), (), s32[]{:S(2)}) async-start(), calls=%async_computation.4 | async-start | bytes 786432 | tf_op jit(solution)/shard_map/reduce_scatter | solution.py:162
  295.9 3.3 copy-start.13
  345.1 7.1 %collective-permute-start = (bf16[16,4096]{1,0:T(8,128)(2,1)S(1)}, bf16[16,4096]{1,0:T(8,128)(2,1)S(1)}, u32[]{:S(2)}, u32[]{:S(2)}) collective-permute-start(bf16[16,4096]{1,0:T(8,128)(2,1)S(1)} %bitcast.149), channel_id=1, source_target_pairs={{0,2},{2,4},{4,6},{6,8},{8,10},{10,12},{12,14},{14,16},{16,18},{18... | collective-permute-start | bytes 393224 | tf_op jit(solution)/shard_map/ppermute | solution.py:157
  352.2 7.1 %collective-permute-start.1 = (bf16[16,4096]{1,0:T(8,128)(2,1)S(1)}, bf16[16,4096]{1,0:T(8,128)(2,1)S(1)}, u32[]{:S(2)}, u32[]{:S(2)}) collective-permute-start(bf16[16,4096]{1,0:T(8,128)(2,1)S(1)} %collective-permute-done), channel_id=1, source_target_pairs={{0,2},{2,4},{4,6},{6,8},{8,10},{10,12},{12,14},{14,16},{16,18},{18... | collective-permute-start | bytes 393224 | tf_op jit(solution)/shard_map/ppermute | solution.py:157
  359.3 7.1 %collective-permute-start.2 = (bf16[16,4096]{1,0:T(8,128)(2,1)S(1)}, bf16[16,4096]{1,0:T(8,128)(2,1)S(1)}, u32[]{:S(2)}, u32[]{:S(2)}) collective-permute-start(bf16[16,4096]{1,0:T(8,128)(2,1)S(1)} %collective-permute-done.1), channel_id=1, source_target_pairs={{0,2},{2,4},{4,6},{6,8},{8,10},{10,12},{12,14},{14,16},{16,18},{18... | collective-permute-start | bytes 393224 | tf_op jit(solution)/shard_map/ppermute | solution.py:157
  366.4 7.1 %collective-permute-start.3 = (bf16[16,4096]{1,0:T(8,128)(2,1)S(1)}, bf16[16,4096]{1,0:T(8,128)(2,1)S(1)}, u32[]{:S(2)}, u32[]{:S(2)}) collective-permute-start(bf16[16,4096]{1,0:T(8,128)(2,1)S(1)} %collective-permute-done.2), channel_id=1, source_target_pairs={{0,2},{2,4},{4,6},{6,8},{8,10},{10,12},{12,14},{14,16},{16,18},{18... | collective-permute-start | bytes 393224 | tf_op jit(solution)/shard_map/ppermute | solution.py:157
  373.5 7.1 %collective-permute-start.4 = (bf16[16,4096]{1,0:T(8,128)(2,1)S(1)}, bf16[16,4096]{1,0:T(8,128)(2,1)S(1)}, u32[]{:S(2)}, u32[]{:S(2)}) collective-permute-start(bf16[16,4096]{1,0:T(8,128)(2,1)S(1)} %collective-permute-done.3), channel_id=1, source_target_pairs={{0,2},{2,4},{4,6},{6,8},{8,10},{10,12},{12,14},{14,16},{16,18},{18... | collective-permute-start | bytes 393224 | tf_op jit(solution)/shard_map/ppermute | solution.py:157
  380.6 7.1 %collective-permute-start.5 = (bf16[16,4096]{1,0:T(8,128)(2,1)S(1)}, bf16[16,4096]{1,0:T(8,128)(2,1)S(1)}, u32[]{:S(2)}, u32[]{:S(2)}) collective-permute-start(bf16[16,4096]{1,0:T(8,128)(2,1)S(1)} %collective-permute-done.4), channel_id=1, source_target_pairs={{0,2},{2,4},{4,6},{6,8},{8,10},{10,12},{12,14},{14,16},{16,18},{18... | collective-permute-start | bytes 393224 | tf_op jit(solution)/shard_map/ppermute | solution.py:157
  387.7 7.1 %collective-permute-start.6 = (bf16[16,4096]{1,0:T(8,128)(2,1)S(1)}, bf16[16,4096]{1,0:T(8,128)(2,1)S(1)}, u32[]{:S(2)}, u32[]{:S(2)}) collective-permute-start(bf16[16,4096]{1,0:T(8,128)(2,1)S(1)} %collective-permute-done.5), channel_id=1, source_target_pairs={{0,2},{2,4},{4,6},{6,8},{8,10},{10,12},{12,14},{14,16},{16,18},{18... | collective-permute-start | bytes 393224 | tf_op jit(solution)/shard_map/ppermute | solution.py:157
  394.8 7.1 %collective-permute-start.7 = (bf16[16,4096]{1,0:T(8,128)(2,1)S(1)}, bf16[16,4096]{1,0:T(8,128)(2,1)S(1)}, u32[]{:S(2)}, u32[]{:S(2)}) collective-permute-start(bf16[16,4096]{1,0:T(8,128)(2,1)S(1)} %collective-permute-done.6), channel_id=1, source_target_pairs={{0,2},{2,4},{4,6},{6,8},{8,10},{10,12},{12,14},{14,16},{16,18},{18... | collective-permute-start | bytes 393224 | tf_op jit(solution)/shard_map/ppermute | solution.py:157
  401.9 7.1 %collective-permute-start.8 = (bf16[16,4096]{1,0:T(8,128)(2,1)S(1)}, bf16[16,4096]{1,0:T(8,128)(2,1)S(1)}, u32[]{:S(2)}, u32[]{:S(2)}) collective-permute-start(bf16[16,4096]{1,0:T(8,128)(2,1)S(1)} %collective-permute-done.7), channel_id=1, source_target_pairs={{0,2},{2,4},{4,6},{6,8},{8,10},{10,12},{12,14},{14,16},{16,18},{18... | collective-permute-start | bytes 393224 | tf_op jit(solution)/shard_map/ppermute | solution.py:157
  409.0 7.1 %collective-permute-start.9 = (bf16[16,4096]{1,0:T(8,128)(2,1)S(1)}, bf16[16,4096]{1,0:T(8,128)(2,1)S(1)}, u32[]{:S(2)}, u32[]{:S(2)}) collective-permute-start(bf16[16,4096]{1,0:T(8,128)(2,1)S(1)} %collective-permute-done.8), channel_id=1, source_target_pairs={{0,2},{2,4},{4,6},{6,8},{8,10},{10,12},{12,14},{14,16},{16,18},{18... | collective-permute-start | bytes 393224 | tf_op jit(solution)/shard_map/ppermute | solution.py:157
  416.0 7.1 %collective-permute-start.10 = (bf16[16,4096]{1,0:T(8,128)(2,1)S(1)}, bf16[16,4096]{1,0:T(8,128)(2,1)S(1)}, u32[]{:S(2)}, u32[]{:S(2)}) collective-permute-start(bf16[16,4096]{1,0:T(8,128)(2,1)S(1)} %collective-permute-done.9), channel_id=1, source_target_pairs={{0,2},{2,4},{4,6},{6,8},{8,10},{10,12},{12,14},{14,16},{16,18},{18... | collective-permute-start | bytes 393224 | tf_op jit(solution)/shard_map/ppermute | solution.py:157
  423.1 7.1 %collective-permute-start.11 = (bf16[16,4096]{1,0:T(8,128)(2,1)S(1)}, bf16[16,4096]{1,0:T(8,128)(2,1)S(1)}, u32[]{:S(2)}, u32[]{:S(2)}) collective-permute-start(bf16[16,4096]{1,0:T(8,128)(2,1)S(1)} %collective-permute-done.10), channel_id=1, source_target_pairs={{0,2},{2,4},{4,6},{6,8},{8,10},{10,12},{12,14},{14,16},{16,18},{18... | collective-permute-start | bytes 393224 | tf_op jit(solution)/shard_map/ppermute | solution.py:157
  430.2 7.1 %collective-permute-start.12 = (bf16[16,4096]{1,0:T(8,128)(2,1)S(1)}, bf16[16,4096]{1,0:T(8,128)(2,1)S(1)}, u32[]{:S(2)}, u32[]{:S(2)}) collective-permute-start(bf16[16,4096]{1,0:T(8,128)(2,1)S(1)} %collective-permute-done.11), channel_id=1, source_target_pairs={{0,2},{2,4},{4,6},{6,8},{8,10},{10,12},{12,14},{14,16},{16,18},{18... | collective-permute-start | bytes 393224 | tf_op jit(solution)/shard_map/ppermute | solution.py:157
  437.3 7.1 %collective-permute-start.13 = (bf16[16,4096]{1,0:T(8,128)(2,1)S(1)}, bf16[16,4096]{1,0:T(8,128)(2,1)S(1)}, u32[]{:S(2)}, u32[]{:S(2)}) collective-permute-start(bf16[16,4096]{1,0:T(8,128)(2,1)S(1)} %collective-permute-done.12), channel_id=1, source_target_pairs={{0,2},{2,4},{4,6},{6,8},{8,10},{10,12},{12,14},{14,16},{16,18},{18... | collective-permute-start | bytes 393224 | tf_op jit(solution)/shard_map/ppermute | solution.py:157
  444.4 7.1 %collective-permute-start.14 = (bf16[16,4096]{1,0:T(8,128)(2,1)S(1)}, bf16[16,4096]{1,0:T(8,128)(2,1)S(1)}, u32[]{:S(2)}, u32[]{:S(2)}) collective-permute-start(bf16[16,4096]{1,0:T(8,128)(2,1)S(1)} %collective-permute-done.13), channel_id=1, source_target_pairs={{0,2},{2,4},{4,6},{6,8},{8,10},{10,12},{12,14},{14,16},{16,18},{18... | collective-permute-start | bytes 393224 | tf_op jit(solution)/shard_map/ppermute | solution.py:157
  444.4 7.8 %copy-start.22 = (bf16[4096,512]{1,0:T(8,128)(2,1)S(1)}, bf16[4096,512]{1,0:T(8,128)(2,1)}, u32[]{:S(2)}) copy-start(bf16[4096,512]{1,0:T(8,128)(2,1)} %param.13) | copy-start | bytes 12582916
  452.1 15.8 %copy-start.1 = (bf16[512,512]{1,0:T(8,128)(2,1)S(1)}, bf16[512,512]{1,0:T(8,128)(2,1)}, u32[]{:S(2)}) copy-start(bf16[512,512]{1,0:T(8,128)(2,1)} %param.11) | copy-start | bytes 1572868
Sparse Core Ops, SparseCore 0:
  16.2 119.6 all-reduce.3
  214.9 52.9 reduce-scatter.9
  271.8 71.8 reduce-scatter.5
  454.4 11.8 reduce-scatter.7
